TPU v7x, 128 devices: a whole 4x4x4 slice. The times are simulated.
128 devices in a mesh: lon: 32 (over y, z, x_lo), chan: 4 (over x_hi, core).
Axes of the slice: x: 4 (x_hi: 2, x_lo: 2; x = x_hi * 2 + x_lo), y: 4, z: 4, core: 2. Of those that a mesh axis runs over, the one named last changes fastest.
Arguments:
- fields: bfloat16 [1440, 49152], P('lon', 'chan'), may hold values from -6 to 6
- mix_weight: bfloat16 [384, 3456], P('chan'), may hold values from -0.109375 to 0.109375
- basis_values: float32 [5, 9, 65, 128], replicated, may hold values from -0.4 to 0.4
- source_rows: int32 [128, 5], replicated, may hold values from 0 to 131, as said below
- lon_reach: int32 [128, 5], replicated, may hold values from 1 to 32, as said below
- quad_weights: float32 [128], replicated, may hold values from 0.2 to 2
Outputs:
- spectrum: float32 [128, 552960], P('lon', 'chan')
Inputs may be any that keep to these rules, and one draw needn't show every extreme that they name: source_rows[i, e] lies between i + 4 - 4 and i + 8; entry 0 of row i is i + 4 and entry 1 is i + 4 - 4. `lon_reach`: every entry of the rows under 4 has reach 32.
All inputs are finite; a program needn't handle non-finite values.
Results may differ from a plain program's by a relative error of at most 0.005.
Values may be sent and summed in bfloat16 or wider, within the bound.
A program may use at most 128 MiB of HBM per device.

v0:
```python
import math
import jax
import jax.numpy as jnp
from jax import lax
from jax.sharding import PartitionSpec as P

C = 384
MODES = 720
K = 9
POLE = 4


def passed_along(value, axis, steps):
    count = lax.axis_size(axis)
    pairs = [(source, (source + steps) % count) for source in range(count)]
    return lax.ppermute(value, axis, pairs)


def extended(block, sides, width):
    for axis, dim in sides:
        count = lax.axis_size(axis)
        forward = [(i, i + 1) for i in range(count - 1)]
        forward.append((count - 1, 0))
        backward = [(target, source) for source, target in forward]
        low = lax.ppermute(
            lax.slice_in_dim(block, block.shape[dim] - width, None, axis=dim), axis, forward
        )
        high = lax.ppermute(lax.slice_in_dim(block, 0, width, axis=dim), axis, backward)
        block = jnp.concatenate([low, block, high], axis=dim)
    return block


def copy_for_each(value, axis):
    copies = jnp.broadcast_to(value, (lax.axis_size(axis), *value.shape))
    return lax.all_to_all(copies, axis, split_axis=0, concat_axis=0, tiled=True)


def joined_along(pieces, dim):
    shape = list(pieces.shape[1:])
    shape[dim] *= pieces.shape[0]
    return jnp.moveaxis(pieces, 0, dim).reshape(shape)


def collect(value, axis, dim):
    pieces = copy_for_each(value, axis)
    return joined_along(pieces, dim)


def extend(field, margin):
    cap_rows = field[:POLE]
    opposite = passed_along(cap_rows, "lon", lax.axis_size("lon") // 2)
    stacked = jnp.concatenate([opposite[::-1], field], axis=0)
    return extended(stacked, (("lon", 1),), margin)


def transform(block):
    length = block.shape[1]
    products = (
        jnp.arange(length, dtype=jnp.int32)[:, None]
        * jnp.arange(MODES, dtype=jnp.int32)[None, :]
        % length
    )
    angle = products.astype(jnp.float32) * (2.0 * math.pi / length)
    factor = 1.0 / math.sqrt(length)
    table = jnp.concatenate([jnp.cos(angle) * factor, -jnp.sin(angle) * factor], axis=1)
    table_high = table.astype(jnp.bfloat16)
    table_low = (table - table_high.astype(jnp.float32)).astype(jnp.bfloat16)
    first = jnp.einsum("rnc,nm->rcm", block, table_high, preferred_element_type=jnp.float32)
    second = jnp.einsum("rnc,nm->rcm", block, table_low, preferred_element_type=jnp.float32)
    return first + second


def shards(fields, mix_weight, basis_values, source_rows, lon_reach, quad_weights):
    lanes = basis_values.shape[2]
    margin = lanes // 2
    row_count = basis_values.shape[3]
    slab = fields.shape[0]
    own_channels = fields.shape[1] // row_count
    local = fields.reshape(slab, own_channels, row_count)
    padded = extend(local.transpose(2, 0, 1), margin)
    weight_whole = collect(mix_weight, "chan", 0)
    weight_cube = weight_whole.reshape(C, K, C)
    weight_part = lax.dynamic_slice_in_dim(
        weight_cube, lax.axis_index("chan") * own_channels, own_channels, 2
    )
    weight_used = weight_part.transpose(1, 2, 0)
    quad_ext = jnp.concatenate([quad_weights[:POLE][::-1], quad_weights], axis=0)
    row_quad = jnp.take(quad_ext, source_rows, axis=0)
    offsets = jnp.arange(lanes, dtype=jnp.int32) - margin
    keeping = jnp.abs(offsets)[None, None, :] <= lon_reach[:, :, None]
    basis_rows = basis_values.transpose(3, 0, 1, 2)
    weighted = basis_rows * row_quad[:, :, None, None]
    filters = jnp.where(keeping[:, :, None, :], weighted, jnp.zeros_like(weighted)).astype(
        jnp.bfloat16
    )
    padded_len = padded.shape[1]
    tap_ids = jnp.arange(lanes, dtype=jnp.int32)[:, None, None]
    source_ids = jnp.arange(padded_len, dtype=jnp.int32)[None, :, None]
    target_ids = jnp.arange(slab, dtype=jnp.int32)[None, None, :]
    selector = (source_ids - target_ids == tap_ids).astype(jnp.bfloat16)
    group = 4
    groups = row_count // group

    def one_group(index):
        start = index * group
        group_rows = lax.dynamic_slice_in_dim(source_rows, start, group, 0)
        group_filters = lax.dynamic_slice_in_dim(filters, start, group, 0)
        picked = jnp.take(padded, group_rows, axis=0)
        banded = jnp.einsum(
            "gekt,tpj->gekpj", group_filters, selector, preferred_element_type=jnp.float32
        ).astype(jnp.bfloat16)
        filtered = jnp.einsum(
            "gepc,gekpj->gkjc", picked, banded, preferred_element_type=jnp.float32
        ).astype(jnp.bfloat16)
        return jnp.einsum(
            "gkjc,kco->gjo", filtered, weight_used, preferred_element_type=jnp.float32
        )

    mixed_terms = lax.map(one_group, jnp.arange(groups, dtype=jnp.int32))
    mixed_terms = mixed_terms.reshape(row_count, slab, mixed_terms.shape[3])
    mixed = lax.psum_scatter(mixed_terms, "chan", scatter_dimension=2, tiled=True).astype(
        jnp.bfloat16
    )
    result = transform(lax.all_to_all(mixed, "lon", split_axis=0, concat_axis=1, tiled=True))
    return result.reshape(result.shape[0], result.shape[1] * result.shape[2])


def solution(mesh):
    placed = (P("lon", "chan"), P("chan", None), P(), P(), P(), P())
    return jax.shard_map(
        shards, mesh=mesh, in_specs=placed, out_specs=P("lon", "chan"), check_vma=False
    )
```

profile of v0, /device:TPU:0, one launch (start us, length us, event | category | flops | bytes accessed | tf_op | source)
XLA Modules:
  0.0 694.8 jit_solution(7724881797279448650)
XLA Ops:
  13.7 4.6 all-to-all-start
  18.9 4.3 gather_fusion.1
  24.0 4.0 rev.7
  37.6 4.8 collective-permute-start.2
  43.1 6.7 copy.78
  50.8 4.2 fusion.39
  55.0 22.2 %collective-permute-done.1 = bf16[132,32,96]{2,1,0:T(8,128)(2,1)} collective-permute-done((bf16[132,32,96]{2,1,0:T(8,128)(2,1)S(1)}, bf16[132,32,96]{2,1,0:T(8,128)(2,1)}, u32[]{:S(2)}, u32[]{:S(2)}) %collective-permute-start.1) | collective-permute-done | bytes 811040 | tf_op jit(solution)/shard_map/ppermute | solution.py:25
  80.1 16.1 %collective-permute-done.2 = bf16[132,32,96]{2,1,0:T(8,128)(2,1)} collective-permute-done((bf16[132,32,96]{2,1,0:T(8,128)(2,1)}, bf16[132,32,96]{2,1,0:T(8,128)(2,1)}, u32[]{:S(2)}, u32[]{:S(2)}) %collective-permute-start.2) | collective-permute-done | bytes 811040 | tf_op jit(solution)/shard_map/ppermute | solution.py:28
  99.1 5.8 pad_maximum_fusion.1
  104.9 8.0 %copy.90 = bf16[132,109,96]{2,1,0:T(8,128)(2,1)} copy(bf16[132,109,96]{0,2,1:T(8,128)(2,1)} %pad_maximum_fusion.1) | data formatting | bytes 5524992
  112.9 5.9 copy.88
  123.4 414.6 %while.11 = (s32[]{:T(128)}, f32[32,4,45,384]{3,2,1,0:T(8,128)}, s32[32]{0:T(128)S(1)}, bf16[128,5,9,65]{3,2,1,0:T(8,128)(2,1)}, s32[128,5]{1,0:T(8,128)}, /*ind...) while((s32[]{:T(128)}, f32[32,4,45,384]{3,2,1,0:T(8,128)}, ...), condition=%wide.region_1.2_spmd.clone, body=%wide.region_0.1_spmd.clone.sunk | while | flops 405619648 | bytes 8615271 | solution.py:119
  210.2 4.0 fusion.70
  287.9 4.0 fusion.70
  430.4 3.9 fusion.70
  482.2 4.0 fusion.70
  508.2 3.9 fusion.70
  538.1 9.9 %copy.92 = f32[128,45,384]{0,1,2:T(8,128)} copy(f32[128,45,384]{2,1,0:T(8,128)} %bitcast.90) | data formatting | bytes 17694720 | tf_op jit(solution)/shard_map/reshape | solution.py:120
  547.9 85.9 %reduce-scatter.2.cloned.1.call-done = f32[128,45,96]{0,1,2:T(8,128)} async-done(((f32[128,45,384]{0,1,2:T(8,128)}), f32[128,45,96]{0,1,2:T(8,128)}) %reduce-scatter.2.cloned.1.call-update) | async-done | bytes 2211856 | tf_op jit(solution)/shard_map/reduce_scatter | solution.py:121
  638.6 7.5 %all-to-all-start.1 = ((bf16[128,45,96]{2,1,0:T(8,128)(2,1)}), bf16[128,45,96]{2,1,0:T(8,128)(2,1)S(1)}, u32[]{:S(2)}, u32[]{:S(2)}) async-start(bf16[128,45,96]{2,1,0:T(8,128)(2,1)} %copy.94), calls=%async_computation.2 | async-start | bytes 3145728 | tf_op jit(solution)/shard_map/all_to_all | solution.py:124
  646.1 19.9 %negate_multiply_fusion = (f32[1440,720]{1,0:T(8,128)}, f32[1440,720]{1,0:T(8,128)}) fusion(), kind=kLoop, calls=%fused_computation.41 | loop fusion | flops 12441600 | bytes 8294400 | tf_op jit(solution)/shard_map/mul | solution.py:65
  665.9 4.6 all-to-all-done.1
  674.1 5.7 fusion.46
  679.9 4.6 fusion.51
  (307 shorter events, 415.4 us)
Async XLA Ops:
  6.5 5.5 copy-start.1
  8.6 9.7 %copy-start.2 = (s32[128,5]{0,1:T(8,128)S(1)}, s32[128,5]{0,1:T(8,128)}, u32[]{:S(2)}) copy-start(s32[128,5]{0,1:T(8,128)} %param.11) | copy-start | bytes 7684
  8.6 10.1 %copy-start.4 = (f32[128]{0:T(128)S(1)}, f32[128]{0:T(128)}, u32[]{:S(2)}) copy-start(f32[128]{0:T(128)} %param.13) | copy-start | bytes 1540
  8.6 14.8 %collective-permute-start = (bf16[4,45,96]{2,0,1:T(4,128)(2,1)S(1)}, bf16[4,45,96]{2,0,1:T(4,128)(2,1)S(1)}, u32[]{:S(2)}, u32[]{:S(2)}) collective-permute-start(bf16[4,45,96]{2,0,1:T(4,128)(2,1)S(1)} %copy.82), channel_id=1, source_target_pairs={{0,64},{4,68},{8,72},{12,76},{16,80},{20,84},{24,88},{28,92},{32,9... | collective-permute-start | bytes 103688 | tf_op jit(solution)/shard_map/ppermute | solution.py:16
  13.7 99.2 %all-to-all-start = ((bf16[4,96,3456]{2,1,0:T(8,128)(2,1)}), bf16[4,96,3456]{2,1,0:T(8,128)(2,1)}, u32[]{:S(2)}, u32[]{:S(2)}) async-start(bf16[4,96,3456]{2,1,0:T(8,128)(2,1)} %broadcast_in_dim.55), calls=%async_computation | async-start | bytes 5308416 | tf_op jit(solution)/shard_map/all_to_all | solution.py:35
  18.3 615.6 %reduce-scatter.2.cloned.1.call-start = ((), (), s32[]{:S(2)}) async-start(), calls=%async_computation.3 | async-start | bytes 11796480 | tf_op jit(solution)/shard_map/reduce_scatter | solution.py:121
  33.1 44.1 %collective-permute-start.1 = (bf16[132,32,96]{2,1,0:T(8,128)(2,1)S(1)}, bf16[132,32,96]{2,1,0:T(8,128)(2,1)}, u32[]{:S(2)}, u32[]{:S(2)}) collective-permute-start(bf16[132,32,96]{2,1,0:T(8,128)(2,1)S(1)} %copy.84), channel_id=1, source_target_pairs={{0,4},{4,8},{8,12},{12,16},{16,20},{20,24},{24,28},{28,32},{32,36}... | collective-permute-start | bytes 2433032 | tf_op jit(solution)/shard_map/ppermute | solution.py:25
  37.6 12.3 %copy-start.3 = (s32[128,5]{0,1:T(8,128)S(1)}, s32[128,5]{0,1:T(8,128)}, u32[]{:S(2)}) copy-start(s32[128,5]{0,1:T(8,128)} %param.12) | copy-start | bytes 7684
  37.6 58.6 %collective-permute-start.2 = (bf16[132,32,96]{2,1,0:T(8,128)(2,1)}, bf16[132,32,96]{2,1,0:T(8,128)(2,1)}, u32[]{:S(2)}, u32[]{:S(2)}) collective-permute-start(bf16[132,32,96]{2,1,0:T(8,128)(2,1)} %copy.85), channel_id=1, source_target_pairs={{4,0},{8,4},{12,8},{16,12},{20,16},{24,20},{28,24},{32,28},{36,32}... | collective-permute-start | bytes 2433032 | tf_op jit(solution)/shard_map/ppermute | solution.py:28
  638.6 32.0 %all-to-all-start.1 = ((bf16[128,45,96]{2,1,0:T(8,128)(2,1)}), bf16[128,45,96]{2,1,0:T(8,128)(2,1)S(1)}, u32[]{:S(2)}, u32[]{:S(2)}) async-start(bf16[128,45,96]{2,1,0:T(8,128)(2,1)} %copy.94), calls=%async_computation.2 | async-start | bytes 3145728 | tf_op jit(solution)/shard_map/all_to_all | solution.py:124
  671.5 8.4 %slice-start = ((s8[4423680]{0:T(1024)(128)(4,1)}), s8[229376]{0:T(1024)(128)(4,1)S(1)}, s32[]{:S(2)}) async-start(s8[4423680]{0:T(1024)(128)(4,1)} %bitcast.87), calls=%async_computation.4 | async-start | bytes 458752
  673.1 1.0 copy-start
  674.1 5.8 slice-start.1
Sparse Core Ops, SparseCore 0:
  548.1 85.7 reduce-scatter.1
where the time goes:
time: 701 us; the launch traced here: 695 us
  matrix products  262 us (37%)
  local copies, waits for them, and re-layouts  190 us (27%)
  waiting for transfers between devices  129 us (18%)
  other arithmetic  56.1 us (8%)
  starting transfers between devices  21.8 us (3%)
  loops' own time  21.5 us (3%)
  between operations  13.6 us (2%)
    dot_general x32, matrix products, one_group(): jnp.einsum('gekt,tpj->gekpj', group_filters, selector, preferred_element_...  126 us
    dot_general x32, matrix products, one_group(): jnp.einsum('gkjc,kco->gjo', filtered, weight_used, preferred_element_type...  126 us
    gather x64, local copies, waits for them, and re-layouts, one_group(): picked = jnp.take(padded, group_rows, axis=0)  97.4 us
    reduce_scatter x1, waiting for transfers between devices, shards(): lax.psum_scatter(mixed_terms, 'chan', scatter_dimension=2, tiled=True)  85.9 us
    and x32, other arithmetic, one_group(): picked = jnp.take(padded, group_rows, axis=0)  22.2 us
    ppermute x1, waiting for transfers between devices, extended(): lax.ppermute(lax.slice_in_dim(block, block.shape[dim] - width, None, axis...  22.2 us
    another operation x1, loops' own time, shards(): mixed_terms = lax.map(one_group, jnp.arange(groups, dtype=jnp.int32))  21.5 us
    mul x1, other arithmetic, transform(): -jnp.sin(angle) * factor  19.9 us
  transfers between devices with their start and end apart: 6, of which 4 were waited for; matrix products, arithmetic and copies ran while one was open for 10% of the time, Pallas kernels for 0%

commit v1 on v0

--- a/solution.py
+++ b/solution.py
@@ -8,6 +8,12 @@
 MODES = 720
 K = 9
 POLE = 4
+
+
+def trade_parts(x, axis, split, join):
+    shards = jnp.split(x, lax.axis_size(axis), axis=split)
+    received = lax.all_to_all(jnp.stack(shards), axis, 0, 0)
+    return jnp.concatenate(received, axis=join)
 
 
 def passed_along(value, axis, steps):
@@ -121,7 +127,7 @@
     mixed = lax.psum_scatter(mixed_terms, "chan", scatter_dimension=2, tiled=True).astype(
         jnp.bfloat16
     )
-    result = transform(lax.all_to_all(mixed, "lon", split_axis=0, concat_axis=1, tiled=True))
+    result = transform(trade_parts(mixed, "lon", 0, 1))
     return result.reshape(result.shape[0], result.shape[1] * result.shape[2])
 
 

time: 701 us -> 717 us (1.023)
  local copies, waits for them, and re-layouts: 190 us -> 208 us
    unnamed x19 -> x52, local copies, waits for them, and re-layouts: 18.1 us -> 38.5 us
where the time goes in v1:
time: 717 us; the launch traced here: 711 us
  matrix products  262 us (37%)
  local copies, waits for them, and re-layouts  208 us (29%)
  waiting for transfers between devices  127 us (18%)
  other arithmetic  56.2 us (8%)
  starting transfers between devices  21.9 us (3%)
  loops' own time  21.7 us (3%)
  between operations  13.6 us (2%)
    dot_general x32, matrix products, one_group(): jnp.einsum('gekt,tpj->gekpj', group_filters, selector, preferred_element_...  127 us
    dot_general x32, matrix products, one_group(): jnp.einsum('gkjc,kco->gjo', filtered, weight_used, preferred_element_type...  126 us
    gather x64, local copies, waits for them, and re-layouts, one_group(): picked = jnp.take(padded, group_rows, axis=0)  97.4 us
    reduce_scatter x1, waiting for transfers between devices, shards(): lax.psum_scatter(mixed_terms, 'chan', scatter_dimension=2, tiled=True)  86 us
    unnamed x52, local copies, waits for them, and re-layouts  38.5 us
    and x32, other arithmetic, one_group(): picked = jnp.take(padded, group_rows, axis=0)  22.2 us
    ppermute x1, waiting for transfers between devices, extended(): lax.ppermute(lax.slice_in_dim(block, block.shape[dim] - width, None, axis...  22.2 us
    another operation x1, loops' own time, shards(): mixed_terms = lax.map(one_group, jnp.arange(groups, dtype=jnp.int32))  21.7 us
  transfers between devices with their start and end apart: 6, of which 4 were waited for; matrix products, arithmetic and copies ran while one was open for 10% of the time, Pallas kernels for 0%

profile of v1, /device:TPU:0, one launch (start us, length us, event | category | flops | bytes accessed | tf_op | source)
XLA Modules:
  0.0 710.6 jit_solution(9924226695984690097)
XLA Ops:
  13.6 4.7 all-to-all-start
  18.9 4.3 gather_fusion.1
  24.1 4.0 rev.7
  37.6 4.8 collective-permute-start.2
  43.2 6.7 copy.105
  50.9 4.2 fusion.39
  55.1 22.2 %collective-permute-done.1 = bf16[132,32,96]{2,1,0:T(8,128)(2,1)} collective-permute-done((bf16[132,32,96]{2,1,0:T(8,128)(2,1)S(1)}, bf16[132,32,96]{2,1,0:T(8,128)(2,1)}, u32[]{:S(2)}, u32[]{:S(2)}) %collective-permute-start.1) | collective-permute-done | bytes 811040 | tf_op jit(solution)/shard_map/ppermute | solution.py:31
  80.2 16.1 %collective-permute-done.2 = bf16[132,32,96]{2,1,0:T(8,128)(2,1)} collective-permute-done((bf16[132,32,96]{2,1,0:T(8,128)(2,1)}, bf16[132,32,96]{2,1,0:T(8,128)(2,1)}, u32[]{:S(2)}, u32[]{:S(2)}) %collective-permute-start.2) | collective-permute-done | bytes 811040 | tf_op jit(solution)/shard_map/ppermute | solution.py:34
  99.2 5.8 pad_maximum_fusion.1
  105.0 8.0 %copy.117 = bf16[132,109,96]{2,1,0:T(8,128)(2,1)} copy(bf16[132,109,96]{0,2,1:T(8,128)(2,1)} %pad_maximum_fusion.1) | data formatting | bytes 5524992
  113.1 5.9 copy.115
  123.6 415.7 %while.11 = (s32[]{:T(128)}, f32[32,4,45,384]{3,2,1,0:T(8,128)}, s32[32]{0:T(128)S(1)}, bf16[128,5,9,65]{3,2,1,0:T(8,128)(2,1)}, s32[128,5]{1,0:T(8,128)}, /*ind...) while((s32[]{:T(128)}, f32[32,4,45,384]{3,2,1,0:T(8,128)}, ...), condition=%wide.region_1.2_spmd.clone, body=%wide.region_0.1_spmd.clone.sunk | while | flops 405619648 | bytes 8688823 | solution.py:125
  180.7 4.0 convolution_convert_fusion.2
  310.5 4.0 convolution_convert_fusion.2
  336.5 4.0 convolution_convert_fusion.2
  375.5 4.0 convolution_convert_fusion.2
  401.5 4.0 convolution_convert_fusion.2
  492.4 4.0 convolution_convert_fusion.2
  531.4 4.0 convolution_convert_fusion.2
  539.3 9.8 %copy.119 = f32[128,45,384]{0,1,2:T(8,128)} copy(f32[128,45,384]{2,1,0:T(8,128)} %bitcast.217) | data formatting | bytes 17694720 | tf_op jit(solution)/shard_map/reshape | solution.py:126
  549.0 86.0 %reduce-scatter.2.cloned.1.call-done = f32[128,45,96]{0,1,2:T(8,128)} async-done(((f32[128,45,384]{0,1,2:T(8,128)}), f32[128,45,96]{0,1,2:T(8,128)}) %reduce-scatter.2.cloned.1.call-update) | async-done | bytes 2211856 | tf_op jit(solution)/shard_map/reduce_scatter | solution.py:127
  658.0 7.5 %all-to-all-start.1 = ((bf16[32,4,45,96]{3,1,2,0:T(4,128)(2,1)}), bf16[32,4,45,96]{3,1,2,0:T(4,128)(2,1)S(1)}, u32[]{:S(2)}, u32[]{:S(2)}) async-start(bf16[32,4,45,96]{3,1,2,0:T(4,128)(2,1)} %constant_dynamic-update-slice_fusion), calls=%async_computation.2 | async-start | bytes 2949120 | tf_op jit(solution)/shard_map/all_to_all | solution.py:15
  665.5 19.9 %negate_multiply_fusion = (f32[1440,720]{1,0:T(8,128)}, f32[1440,720]{1,0:T(8,128)}) fusion(), kind=kLoop, calls=%fused_computation.41 | loop fusion | flops 12441600 | bytes 8294400 | tf_op jit(solution)/shard_map/mul | solution.py:71
  691.0 5.7 fusion.46
  (402 shorter events, 432.0 us)
Async XLA Ops:
  8.6 14.9 %collective-permute-start = (bf16[4,45,96]{2,0,1:T(4,128)(2,1)S(1)}, bf16[4,45,96]{2,0,1:T(4,128)(2,1)S(1)}, u32[]{:S(2)}, u32[]{:S(2)}) collective-permute-start(bf16[4,45,96]{2,0,1:T(4,128)(2,1)S(1)} %copy.109), channel_id=1, source_target_pairs={{0,64},{4,68},{8,72},{12,76},{16,80},{20,84},{24,88},{28,92},{32,9... | collective-permute-start | bytes 103688 | tf_op jit(solution)/shard_map/ppermute | solution.py:22
  13.6 5.1 copy-start.6
  13.6 99.4 %all-to-all-start = ((bf16[4,96,3456]{2,1,0:T(8,128)(2,1)}), bf16[4,96,3456]{2,1,0:T(8,128)(2,1)}, u32[]{:S(2)}, u32[]{:S(2)}) async-start(bf16[4,96,3456]{2,1,0:T(8,128)(2,1)} %broadcast_in_dim.55), calls=%async_computation | async-start | bytes 5308416 | tf_op jit(solution)/shard_map/all_to_all | solution.py:41
  18.4 616.7 %reduce-scatter.2.cloned.1.call-start = ((), (), s32[]{:S(2)}) async-start(), calls=%async_computation.3 | async-start | bytes 11796480 | tf_op jit(solution)/shard_map/reduce_scatter | solution.py:127
  33.2 44.1 %collective-permute-start.1 = (bf16[132,32,96]{2,1,0:T(8,128)(2,1)S(1)}, bf16[132,32,96]{2,1,0:T(8,128)(2,1)}, u32[]{:S(2)}, u32[]{:S(2)}) collective-permute-start(bf16[132,32,96]{2,1,0:T(8,128)(2,1)S(1)} %copy.111), channel_id=1, source_target_pairs={{0,4},{4,8},{8,12},{12,16},{16,20},{20,24},{24,28},{28,32},{32,36}... | collective-permute-start | bytes 2433032 | tf_op jit(solution)/shard_map/ppermute | solution.py:31
  37.6 58.6 %collective-permute-start.2 = (bf16[132,32,96]{2,1,0:T(8,128)(2,1)}, bf16[132,32,96]{2,1,0:T(8,128)(2,1)}, u32[]{:S(2)}, u32[]{:S(2)}) collective-permute-start(bf16[132,32,96]{2,1,0:T(8,128)(2,1)} %copy.112), channel_id=1, source_target_pairs={{4,0},{8,4},{12,8},{16,12},{20,16},{24,20},{28,24},{32,28},{36,32}... | collective-permute-start | bytes 2433032 | tf_op jit(solution)/shard_map/ppermute | solution.py:34
  43.2 6.8 copy-start.5
  123.6 5.1 copy-start.2
  136.6 5.1 copy-start.2
  175.6 5.1 copy-start.2
  188.6 5.1 copy-start.2
  227.5 5.1 copy-start.2
  305.4 5.1 copy-start.2
  318.4 5.1 copy-start.2
  383.4 5.1 copy-start.2
  396.4 5.1 copy-start.2
  409.4 5.1 copy-start.2
  422.4 5.1 copy-start.2
  513.3 5.1 copy-start.2
  526.3 5.1 copy-start.2
  658.0 30.4 %all-to-all-start.1 = ((bf16[32,4,45,96]{3,1,2,0:T(4,128)(2,1)}), bf16[32,4,45,96]{3,1,2,0:T(4,128)(2,1)S(1)}, u32[]{:S(2)}, u32[]{:S(2)}) async-start(bf16[32,4,45,96]{3,1,2,0:T(4,128)(2,1)} %constant_dynamic-update-slice_fusion), calls=%async_computation.2 | async-start | bytes 2949120 | tf_op jit(solution)/shard_map/all_to_all | solution.py:15
  688.3 8.4 %slice-start = ((s8[4423680]{0:T(1024)(128)(4,1)}), s8[229376]{0:T(1024)(128)(4,1)S(1)}, s32[]{:S(2)}) async-start(s8[4423680]{0:T(1024)(128)(4,1)} %bitcast.214), calls=%async_computation.4 | async-start | bytes 458752
  691.0 5.8 slice-start.1
  691.0 6.1 copy-start
  (22 other events, 106.2 us)
Sparse Core Ops, SparseCore 0:
  549.2 85.7 reduce-scatter.1
